TPU v7x, 128 devices: a whole 4x4x4 slice. The times are simulated.
128 devices in a mesh: seq: 16 (over z, x_hi, core), exp: 8 (over y, x_lo).
Axes of the slice: x: 4 (x_hi: 2, x_lo: 2; x = x_hi * 2 + x_lo), y: 4, z: 4, core: 2. Of those that a mesh axis runs over, the one named last changes fastest.
Arguments:
- tokens: bfloat16 [524288, 1024], P(('seq', 'exp')), may hold values from -6 to 6
- norm_gain: float32 [1024], replicated, may hold values from 0.1 to 1.9
- slot_param: bfloat16 [1024, 256], replicated
- w_in: bfloat16 [64, 1024, 4096], P('exp', None, 'seq'), may hold values from -0.1875 to 0.1875
- w_out: bfloat16 [64, 4096, 1024], P('exp', 'seq'), may hold values from -0.09375 to 0.09375
Outputs:
- mixed: bfloat16 [524288, 1024], P(('seq', 'exp'))
All inputs are finite; a program needn't handle non-finite values.
Results may differ from a plain program's by a relative error of at most 0.02.
The roundings to bfloat16 on the way count: a program that leaves them out, or rounds other values in their place, can miss the bound.
Values may be sent and summed in bfloat16 or wider, within the bound.
A program may use at most 128 MiB of HBM per device.

v0:
```python
import jax
import jax.numpy as jnp
from jax import lax
from jax.sharding import PartitionSpec as P


def on_device(tokens, norm_gain, slot_param, w_in, w_out):
    n_exp = lax.axis_size("exp")
    slot_count = slot_param.shape[1]
    width = tokens.shape[1]
    group = slot_count // n_exp
    values = tokens.astype(jnp.float32)
    scale = lax.rsqrt(jnp.mean(values * values, axis=1, keepdims=True) + 1e-06)
    normed = (values * scale * norm_gain[None, :]).astype(jnp.bfloat16)
    logits = jnp.dot(normed, slot_param, preferred_element_type=jnp.float32)
    col_peak = lax.pmax(jnp.max(logits, axis=0), ("seq", "exp"))
    raw = jnp.exp(logits - col_peak[None, :])
    dispatch = raw.astype(jnp.bfloat16)
    weighted = lax.dot_general(
        dispatch, normed, (((0,), (0,)), ((), ())), preferred_element_type=jnp.float32
    )
    col_total = jnp.sum(raw, axis=0)
    group_sum, group_total = (
        lax.psum_scatter(weighted, "exp", scatter_dimension=0, tiled=True),
        lax.psum_scatter(col_total, "exp", scatter_dimension=0, tiled=True),
    )
    group_sum, group_total = lax.psum((group_sum, group_total), "seq")
    slot_in = (group_sum / group_total[:, None]).astype(jnp.bfloat16)
    local_experts = w_in.shape[0]
    grouped = slot_in.reshape(local_experts, group // local_experts, width)
    first = jnp.einsum("esd,edh->esh", grouped, w_in, preferred_element_type=jnp.float32)
    hidden_act = jax.nn.gelu(first, approximate=False).astype(jnp.bfloat16)
    partial_out = jnp.einsum(
        "esh,ehd->esd", hidden_act, w_out, preferred_element_type=jnp.float32
    ).reshape(group, width)
    group_out = lax.psum(partial_out.astype(jnp.bfloat16), "seq")
    slot_out = lax.all_gather(group_out, "exp", axis=0, tiled=True)
    row_peak = jnp.max(logits, axis=1, keepdims=True)
    expon = jnp.exp(logits - row_peak)
    combine = (expon / jnp.sum(expon, axis=1, keepdims=True)).astype(jnp.bfloat16)
    return jnp.dot(combine, slot_out, preferred_element_type=jnp.float32).astype(jnp.bfloat16)


def solution(mesh):
    in_specs = (P(("seq", "exp"), None), P(), P(), P("exp", None, "seq"), P("exp", "seq", None))
    out_specs = P(("seq", "exp"), None)
    return jax.shard_map(
        on_device, mesh=mesh, in_specs=in_specs, out_specs=out_specs, check_vma=False
    )
```

profile of v0, /device:TPU:0, one launch (start us, length us, event | category | flops | bytes accessed | tf_op | source)
XLA Modules:
  0.0 451.9 jit_solution(9162732727968139499)
XLA Ops:
  6.5 5.2 %fusion = f32[4096]{0:T(1024)S(1)} fusion(bf16[4096,1024]{1,0:T(8,128)(2,1)} %param.5), kind=kLoop, calls=%fused_computation.2 | loop fusion | flops 12578816 | bytes 8404992 | tf_op jit(solution)/shard_map/reduce_sum | solution.py:13
  11.8 0.7 copy-done.1
  12.5 5.2 %fusion.89 = (f32[4096]{0:T(1024)S(1)}, f32[256]{0:T(256)S(1)}, f32[4096,256]{1,0:T(8,128)}) fusion(bf16[1024,256]{1,0:T(8,128)(2,1)S(1)} %copy-done, bf16[4096,1024]{1,0:T(8,128)(2,1)S(1)} %copy-done.1, f32[1024]{0:T(1024)S(1)} %copy-done.3, f32[4096]{0:T(1024)S(1)} %add_rsqrt_fusion), kind=kOutput, calls=%fused_computation.106 | convolution fusion | flops 2166353664 | bytes 13145088 | tf_op jit(solution)/shard_map/dot_general | solution.py:15
  17.7 68.2 %pmax.7 = f32[256]{0:T(256)S(1)} all-reduce(f32[256]{0:T(256)S(1)} %get-tuple-element.8), channel_id=1, replica_groups=mesh['seq'=16,'exp'=8] {'seq','exp'}, use_global_device_ids=true, to_apply=%region_4.0 | all-reduce | flops 256 | bytes 2048 | tf_op jit(solution)/shard_map/pmax | solution.py:16
  85.9 8.9 %fusion.6 = f32[256,1024]{1,0:T(8,128)} fusion(bf16[4096,1024]{1,0:T(8,128)(2,1)} %param.5, f32[1024]{0:T(1024)S(1)} %copy-done.3, f32[4096]{0:T(1024)S(1)} %add_rsqrt_fusion, f32[4096,256]{1,0:T(8,128)} %get-tuple-element.11, f32[256]{0:T(256)S(1)} %pmax.7), kind=kOutput, calls=%fused_computation.12 | convolution fusion | flops 2166358016 | bytes 13652992 | tf_op jit(solution)/shard_map/dot_general | solution.py:19
  94.8 0.0 all-reduce.4.cloned.1.call-start
  94.8 37.9 %reduce-scatter.2.cloned.1.call-done = f32[32,1024]{1,0:T(8,128)} async-done(((f32[256,1024]{1,0:T(8,128)}), f32[32,1024]{1,0:T(8,128)}) %reduce-scatter.2.cloned.1.call-update) | async-done | bytes 131088 | tf_op jit(solution)/shard_map/reduce_scatter | solution.py:24
  132.7 0.0 all-reduce.4.cloned.1.call-update
  132.8 0.0 all-reduce.6.cloned.1.call-start
  132.8 3.4 fusion.3
  136.2 0.6 dynamic-slice
  137.4 16.9 %all-reduce = f32[256]{0:T(256)S(1)} all-reduce(f32[256]{0:T(256)S(1)} %get-tuple-element.6), channel_id=3, replica_groups=mesh['seq'=16,'exp'=8] {'exp'}, use_global_device_ids=true, to_apply=%region_8.0.clone | all-reduce | flops 256 | bytes 2048
  154.4 0.1 dynamic-slice.1
  154.4 33.1 %psum.22 = f32[32]{0:T(128)S(1)} all-reduce(f32[32]{0:T(128)S(1)} %dynamic-slice.1), channel_id=1, replica_groups=mesh['seq'=16,'exp'=8] {'seq'}, use_global_device_ids=true, to_apply=%region_9.0 | all-reduce | flops 32 | bytes 256 | tf_op jit(solution)/shard_map/psum | solution.py:27
  187.6 85.0 %all-reduce.4.cloned.1.call-done = f32[32,1024]{1,0:T(8,128)} async-done(((f32[32,1024]{1,0:T(8,128)}), f32[32,1024]{1,0:T(8,128)}) %all-reduce.4.cloned.1.call-update) | async-done | bytes 131088 | tf_op jit(solution)/shard_map/psum | solution.py:27
  272.5 1.0 divide_convert_fusion.2
  273.6 3.0 fusion.55
  276.6 0.4 copy-done.2
  277.0 0.7 convolution_convert_fusion.1
  277.7 0.7 convert_element_type.34
  278.3 0.0 all-reduce.6.cloned.1.call-update
  278.4 130.1 %all-reduce.6.cloned.1.call-done = bf16[32,1024]{1,0:T(8,128)(2,1)} async-done(((bf16[32,1024]{1,0:T(8,128)(2,1)}), bf16[32,1024]{1,0:T(8,128)(2,1)}) %all-reduce.6.cloned.1.call-update) | async-done | bytes 65552 | tf_op jit(solution)/shard_map/psum | solution.py:36
  408.5 30.5 %all_gather.3 = bf16[256,1024]{1,0:T(8,128)(2,1)S(1)} all-gather(bf16[32,1024]{1,0:T(8,128)(2,1)} %all-reduce.6.cloned.1.call-done), channel_id=1, replica_groups=mesh['seq'=16,'exp'=8] {'exp'}, dimensions={0}, use_global_device_ids=true | all-gather | bytes 589824 | tf_op jit(solution)/shard_map/all_gather | solution.py:37
  439.0 6.4 %convolution_convert_fusion = bf16[4096,1024]{1,0:T(8,128)(2,1)} fusion(bf16[256,1024]{1,0:T(8,128)(2,1)S(1)} %all_gather.3, f32[4096,256]{1,0:T(8,128)} %get-tuple-element.11, f32[4096]{0:T(1024)S(1)} %get-tuple-element.5, f32[4096]{0:T(1024)S(1)} %get-tuple-element.7), kind=kOutput, calls=%fused_computation.5 | convolution fusion | flops 2154823680 | bytes 13139968 | tf_op jit(solution)/shard_map/dot_general | solution.py:41
  (12 shorter events, 0.1 us)
Async XLA Ops:
  6.5 5.3 %copy-start = (bf16[1024,256]{1,0:T(8,128)(2,1)S(1)}, bf16[1024,256]{1,0:T(8,128)(2,1)}, u32[]{:S(2)}) copy-start(bf16[1024,256]{1,0:T(8,128)(2,1)} %param.7) | copy-start | bytes 1572868
  6.5 5.3 %copy-start.3 = (f32[1024]{0:T(1024)S(1)}, f32[1024]{0:T(1024)}, u32[]{:S(2)}) copy-start(f32[1024]{0:T(1024)} %param.6) | copy-start | bytes 12292
  6.5 126.2 %reduce-scatter.2.cloned.1.call-start = ((), (), s32[]{:S(2)}) async-start(), calls=%async_computation.1 | async-start | bytes 1179648 | tf_op jit(solution)/shard_map/reduce_scatter | solution.py:24
  6.5 6.0 %copy-start.1 = (bf16[4096,1024]{1,0:T(8,128)(2,1)S(1)}, bf16[4096,1024]{1,0:T(8,128)(2,1)}, u32[]{:S(2)}) copy-start(bf16[4096,1024]{1,0:T(8,128)(2,1)} %param.5) | copy-start | bytes 25165828
  94.8 41.4 %copy-start.4 = (u32[128]{0:T(128)S(1)}, u32[128]{0:T(128)}, u32[]{:S(2)}) copy-start(u32[128]{0:T(128)} %constant.70) | copy-start | bytes 1540
  94.8 177.8 %all-reduce.4.cloned.1.call-start = ((), (), s32[]{:S(2)}) async-start(), calls=%async_computation.2 | async-start | bytes 262144 | tf_op jit(solution)/shard_map/psum | solution.py:27
  132.8 275.7 %all-reduce.6.cloned.1.call-start = ((), (), s32[]{:S(2)}) async-start(), calls=%async_computation.3 | async-start | bytes 131072 | tf_op jit(solution)/shard_map/psum | solution.py:36
  273.6 3.5 copy-start.2
Sparse Core Ops, SparseCore 0:
  94.9 37.7 reduce-scatter.1
  135.2 137.2 all-reduce.3
  278.5 129.9 all-reduce.5
where the time goes:
time: 452 us
  waiting for transfers between devices  253 us (56%)
  blocking collectives  149 us (33%)
  matrix products  24.2 us (5%)
  between operations  13.8 us (3%)
  other arithmetic  9.59 us (2%)
    psum x1, waiting for transfers between devices, on_device(): group_out = lax.psum(partial_out.astype(jnp.bfloat16), 'seq')  130 us
    psum x1, waiting for transfers between devices, on_device(): group_sum, group_total = lax.psum((group_sum, group_total), 'seq')  85 us
    pmax x1, blocking collectives, on_device(): col_peak = lax.pmax(jnp.max(logits, axis=0), ('seq', 'exp'))  68.2 us
    reduce_scatter x1, waiting for transfers between devices, on_device(): lax.psum_scatter(weighted, 'exp', scatter_dimension=0, tiled=True)  37.9 us
    psum x1, blocking collectives, on_device(): group_sum, group_total = lax.psum((group_sum, group_total), 'seq')  33.1 us
    all_gather x1, blocking collectives, on_device(): slot_out = lax.all_gather(group_out, 'exp', axis=0, tiled=True)  30.5 us
    unnamed x1, blocking collectives  16.9 us
  transfers between devices with their start and end apart: 3, of which 3 were waited for; matrix products, arithmetic and copies ran while one was open for 1% of the time, Pallas kernels for 0%

commit v1 on v0

--- a/solution.py
+++ b/solution.py
@@ -33,7 +33,7 @@
     partial_out = jnp.einsum(
         "esh,ehd->esd", hidden_act, w_out, preferred_element_type=jnp.float32
     ).reshape(group, width)
-    group_out = lax.psum(partial_out.astype(jnp.bfloat16), "seq")
+    group_out = jnp.sum(lax.all_gather(partial_out.astype(jnp.bfloat16), "seq"), axis=0)
     slot_out = lax.all_gather(group_out, "exp", axis=0, tiled=True)
     row_peak = jnp.max(logits, axis=1, keepdims=True)
     expon = jnp.exp(logits - row_peak)

time: 452 us -> 369 us (0.82)
  waiting for transfers between devices: 253 us -> 169 us
    psum x1 -> x0, waiting for transfers between devices: 130 us -> none  [on_device(): group_out = lax.psum(partial_out.astype(jnp.bfloat16), 'seq')]
    all_gather x0 -> x1, waiting for transfers between devices: none -> 46.1 us  [on_device(): lax.all_gather(partial_out.astype(jnp.bfloat16), 'seq')]
where the time goes in v1:
time: 369 us
  waiting for transfers between devices  169 us (46%)
  blocking collectives  148 us (40%)
  matrix products  24.2 us (7%)
  between operations  13.8 us (4%)
  other arithmetic  11 us (3%)
    psum x1, waiting for transfers between devices, on_device(): group_sum, group_total = lax.psum((group_sum, group_total), 'seq')  84.7 us
    pmax x1, blocking collectives, on_device(): col_peak = lax.pmax(jnp.max(logits, axis=0), ('seq', 'exp'))  68.2 us
    all_gather x1, waiting for transfers between devices, on_device(): lax.all_gather(partial_out.astype(jnp.bfloat16), 'seq')  46.1 us
    reduce_scatter x1, waiting for transfers between devices, on_device(): lax.psum_scatter(weighted, 'exp', scatter_dimension=0, tiled=True)  37.9 us
    psum x1, blocking collectives, on_device(): group_sum, group_total = lax.psum((group_sum, group_total), 'seq')  33.1 us
    all_gather x1, blocking collectives, on_device(): slot_out = lax.all_gather(group_out, 'exp', axis=0, tiled=True)  30 us
    unnamed x1, blocking collectives  17 us
    dot_general x1, matrix products, on_device(): lax.dot_general(dispatch, normed, (((0,), (0,)), ((), ())), preferred_ele...  8.92 us
  transfers between devices with their start and end apart: 3, of which 3 were waited for; matrix products, arithmetic and copies ran while one was open for 1% of the time, Pallas kernels for 0%

profile of v1, /device:TPU:0, one launch (start us, length us, event | category | flops | bytes accessed | tf_op | source)
XLA Modules:
  0.0 368.6 jit_solution(2333376561539234682)
XLA Ops:
  6.5 5.2 %fusion = f32[4096]{0:T(1024)S(1)} fusion(bf16[4096,1024]{1,0:T(8,128)(2,1)} %param.5), kind=kLoop, calls=%fused_computation.2 | loop fusion | flops 12578816 | bytes 8404992 | tf_op jit(solution)/shard_map/reduce_sum | solution.py:13
  11.8 0.7 copy-done.1
  12.5 5.2 %fusion.89 = (f32[4096]{0:T(1024)S(1)}, f32[256]{0:T(256)S(1)}, f32[4096,256]{1,0:T(8,128)}) fusion(bf16[1024,256]{1,0:T(8,128)(2,1)S(1)} %copy-done, bf16[4096,1024]{1,0:T(8,128)(2,1)S(1)} %copy-done.1, f32[1024]{0:T(1024)S(1)} %copy-done.3, f32[4096]{0:T(1024)S(1)} %add_rsqrt_fusion), kind=kOutput, calls=%fused_computation.106 | convolution fusion | flops 2166353664 | bytes 13145088 | tf_op jit(solution)/shard_map/dot_general | solution.py:15
  17.7 68.2 %pmax.7 = f32[256]{0:T(256)S(1)} all-reduce(f32[256]{0:T(256)S(1)} %get-tuple-element.8), channel_id=1, replica_groups=mesh['seq'=16,'exp'=8] {'seq','exp'}, use_global_device_ids=true, to_apply=%region_4.0 | all-reduce | flops 256 | bytes 2048 | tf_op jit(solution)/shard_map/pmax | solution.py:16
  85.9 8.9 %fusion.6 = f32[256,1024]{1,0:T(8,128)} fusion(bf16[4096,1024]{1,0:T(8,128)(2,1)} %param.5, f32[1024]{0:T(1024)S(1)} %copy-done.3, f32[4096]{0:T(1024)S(1)} %add_rsqrt_fusion, f32[4096,256]{1,0:T(8,128)} %get-tuple-element.11, f32[256]{0:T(256)S(1)} %pmax.7), kind=kOutput, calls=%fused_computation.12 | convolution fusion | flops 2166358016 | bytes 13652992 | tf_op jit(solution)/shard_map/dot_general | solution.py:19
  94.8 0.0 all-reduce.3.cloned.1.call-start
  94.9 37.9 %reduce-scatter.2.cloned.1.call-done = f32[32,1024]{1,0:T(8,128)} async-done(((f32[256,1024]{1,0:T(8,128)}), f32[32,1024]{1,0:T(8,128)}) %reduce-scatter.2.cloned.1.call-update) | async-done | bytes 131088 | tf_op jit(solution)/shard_map/reduce_scatter | solution.py:24
  132.7 0.0 all-reduce.3.cloned.1.call-update
  132.8 0.0 all-gather.2.cloned.1.call-start
  132.8 3.4 fusion.3
  136.2 0.6 dynamic-slice
  137.4 17.0 %all-reduce = f32[256]{0:T(256)S(1)} all-reduce(f32[256]{0:T(256)S(1)} %get-tuple-element.6), channel_id=3, replica_groups=mesh['seq'=16,'exp'=8] {'exp'}, use_global_device_ids=true, to_apply=%region_8.0.clone | all-reduce | flops 256 | bytes 2048
  154.4 0.1 dynamic-slice.1
  154.5 33.1 %psum.15 = f32[32]{0:T(128)S(1)} all-reduce(f32[32]{0:T(128)S(1)} %dynamic-slice.1), channel_id=1, replica_groups=mesh['seq'=16,'exp'=8] {'seq'}, use_global_device_ids=true, to_apply=%region_9.0 | all-reduce | flops 32 | bytes 256 | tf_op jit(solution)/shard_map/psum | solution.py:27
  187.6 84.7 %all-reduce.3.cloned.1.call-done = f32[32,1024]{1,0:T(8,128)} async-done(((f32[32,1024]{1,0:T(8,128)}), f32[32,1024]{1,0:T(8,128)}) %all-reduce.3.cloned.1.call-update) | async-done | bytes 131088 | tf_op jit(solution)/shard_map/psum | solution.py:27
  272.4 1.0 divide_convert_fusion.2
  273.4 3.0 fusion.55
  276.4 0.4 copy-done.2
  276.8 0.7 convolution_convert_fusion.1
  277.5 0.7 convert_element_type.43
  278.2 46.1 %all-gather.2.cloned.1.call-done = bf16[16,32,1024]{2,1,0:T(8,128)(2,1)} async-done(((bf16[1,32,1024]{2,1,0:T(8,128)(2,1)}), bf16[16,32,1024]{2,1,0:T(8,128)(2,1)}) %all-gather.2.cloned.1.call-update) | async-done | bytes 1048592 | tf_op jit(solution)/shard_map/all_gather | solution.py:36
  324.3 1.4 reduce_sum.42
  325.7 30.0 %all_gather.8 = bf16[256,1024]{1,0:T(8,128)(2,1)S(1)} all-gather(bf16[32,1024]{1,0:T(8,128)(2,1)S(1)} %reduce_sum.42), channel_id=1, replica_groups=mesh['seq'=16,'exp'=8] {'exp'}, dimensions={0}, use_global_device_ids=true | all-gather | bytes 589824 | tf_op jit(solution)/shard_map/all_gather | solution.py:37
  355.7 6.4 %convolution_convert_fusion = bf16[4096,1024]{1,0:T(8,128)(2,1)} fusion(bf16[256,1024]{1,0:T(8,128)(2,1)S(1)} %all_gather.8, f32[4096,256]{1,0:T(8,128)} %get-tuple-element.11, f32[4096]{0:T(1024)S(1)} %get-tuple-element.5, f32[4096]{0:T(1024)S(1)} %get-tuple-element.7), kind=kOutput, calls=%fused_computation.5 | convolution fusion | flops 2154823680 | bytes 13139968 | tf_op jit(solution)/shard_map/dot_general | solution.py:41
  (13 shorter events, 0.1 us)
Async XLA Ops:
  6.5 5.3 %copy-start = (bf16[1024,256]{1,0:T(8,128)(2,1)S(1)}, bf16[1024,256]{1,0:T(8,128)(2,1)}, u32[]{:S(2)}) copy-start(bf16[1024,256]{1,0:T(8,128)(2,1)} %param.7) | copy-start | bytes 1572868
  6.5 5.3 %copy-start.3 = (f32[1024]{0:T(1024)S(1)}, f32[1024]{0:T(1024)}, u32[]{:S(2)}) copy-start(f32[1024]{0:T(1024)} %param.6) | copy-start | bytes 12292
  6.5 126.2 %reduce-scatter.2.cloned.1.call-start = ((), (), s32[]{:S(2)}) async-start(), calls=%async_computation.1 | async-start | bytes 1179648 | tf_op jit(solution)/shard_map/reduce_scatter | solution.py:24
  6.5 6.0 %copy-start.1 = (bf16[4096,1024]{1,0:T(8,128)(2,1)S(1)}, bf16[4096,1024]{1,0:T(8,128)(2,1)}, u32[]{:S(2)}) copy-start(bf16[4096,1024]{1,0:T(8,128)(2,1)} %param.5) | copy-start | bytes 25165828
  94.8 41.4 %copy-start.4 = (u32[128]{0:T(128)S(1)}, u32[128]{0:T(128)}, u32[]{:S(2)}) copy-start(u32[128]{0:T(128)} %constant.72) | copy-start | bytes 1540
  94.8 177.5 %all-reduce.3.cloned.1.call-start = ((), (), s32[]{:S(2)}) async-start(), calls=%async_computation.2 | async-start | bytes 262144 | tf_op jit(solution)/shard_map/psum | solution.py:27
  132.8 191.5 %all-gather.2.cloned.1.call-start = ((), (), s32[]{:S(2)}) async-start(), calls=%async_computation.3 | async-start | bytes 1114112 | tf_op jit(solution)/shard_map/all_gather | solution.py:36
  273.4 3.5 copy-start.2
Sparse Core Ops, SparseCore 0:
  94.9 37.7 reduce-scatter.1
  135.2 137.1 all-reduce.2
  278.3 45.9 all-gather.1

commit v2 on v0

--- a/solution.py
+++ b/solution.py
@@ -34,7 +34,9 @@
         "esh,ehd->esd", hidden_act, w_out, preferred_element_type=jnp.float32
     ).reshape(group, width)
     group_out = lax.psum(partial_out.astype(jnp.bfloat16), "seq")
-    slot_out = lax.all_gather(group_out, "exp", axis=0, tiled=True)
+    slot_out = jnp.concatenate(
+        lax.all_to_all(jnp.stack([group_out] * lax.axis_size("exp")), "exp", 0, 0), axis=0
+    )
     row_peak = jnp.max(logits, axis=1, keepdims=True)
     expon = jnp.exp(logits - row_peak)
     combine = (expon / jnp.sum(expon, axis=1, keepdims=True)).astype(jnp.bfloat16)

time: 452 us -> 436 us (0.965)
  blocking collectives: 149 us -> 132 us
    all_gather x1 -> x0, blocking collectives: 30.5 us -> none  [on_device(): slot_out = lax.all_gather(group_out, 'exp', axis=0, tiled=True)]
    all_to_all x0 -> x1, blocking collectives: none -> 13.8 us  [on_device(): lax.all_to_all(jnp.stack([group_out] * lax.axis_size('exp')), 'exp', 0, 0)]
where the time goes in v2:
time: 436 us
  waiting for transfers between devices  253 us (58%)
  blocking collectives  132 us (30%)
  matrix products  24.2 us (6%)
  between operations  13.8 us (3%)
  other arithmetic  9.59 us (2%)
    psum x1, waiting for transfers between devices, on_device(): group_out = lax.psum(partial_out.astype(jnp.bfloat16), 'seq')  130 us
    psum x1, waiting for transfers between devices, on_device(): group_sum, group_total = lax.psum((group_sum, group_total), 'seq')  85 us
    pmax x1, blocking collectives, on_device(): col_peak = lax.pmax(jnp.max(logits, axis=0), ('seq', 'exp'))  68.2 us
    reduce_scatter x1, waiting for transfers between devices, on_device(): lax.psum_scatter(weighted, 'exp', scatter_dimension=0, tiled=True)  37.9 us
    psum x1, blocking collectives, on_device(): group_sum, group_total = lax.psum((group_sum, group_total), 'seq')  33.1 us
    unnamed x1, blocking collectives  16.9 us
    all_to_all x1, blocking collectives, on_device(): lax.all_to_all(jnp.stack([group_out] * lax.axis_size('exp')), 'exp', 0, 0)  13.8 us
    dot_general x1, matrix products, on_device(): lax.dot_general(dispatch, normed, (((0,), (0,)), ((), ())), preferred_ele...  8.9 us
  transfers between devices with their start and end apart: 3, of which 3 were waited for; matrix products, arithmetic and copies ran while one was open for 1% of the time, Pallas kernels for 0%

profile of v2, /device:TPU:0, one launch (start us, length us, event | category | flops | bytes accessed | tf_op | source)
XLA Modules:
  0.0 436.1 jit_solution(12407074653752215523)
XLA Ops:
  6.5 5.2 %fusion = f32[4096]{0:T(1024)S(1)} fusion(bf16[4096,1024]{1,0:T(8,128)(2,1)} %param.5), kind=kLoop, calls=%fused_computation.2 | loop fusion | flops 12578816 | bytes 8404992 | tf_op jit(solution)/shard_map/reduce_sum | solution.py:13
  11.8 0.7 copy-done.1
  12.5 5.2 %fusion.89 = (f32[4096]{0:T(1024)S(1)}, f32[256]{0:T(256)S(1)}, f32[4096,256]{1,0:T(8,128)}) fusion(bf16[1024,256]{1,0:T(8,128)(2,1)S(1)} %copy-done, bf16[4096,1024]{1,0:T(8,128)(2,1)S(1)} %copy-done.1, f32[1024]{0:T(1024)S(1)} %copy-done.3, f32[4096]{0:T(1024)S(1)} %add_rsqrt_fusion), kind=kOutput, calls=%fused_computation.106 | convolution fusion | flops 2166353664 | bytes 13145088 | tf_op jit(solution)/shard_map/dot_general | solution.py:15
  17.7 68.2 %pmax.7 = f32[256]{0:T(256)S(1)} all-reduce(f32[256]{0:T(256)S(1)} %get-tuple-element.8), channel_id=1, replica_groups=mesh['seq'=16,'exp'=8] {'seq','exp'}, use_global_device_ids=true, to_apply=%region_4.0 | all-reduce | flops 256 | bytes 2048 | tf_op jit(solution)/shard_map/pmax | solution.py:16
  85.9 8.9 %fusion.6 = f32[256,1024]{1,0:T(8,128)} fusion(bf16[4096,1024]{1,0:T(8,128)(2,1)} %param.5, f32[1024]{0:T(1024)S(1)} %copy-done.3, f32[4096]{0:T(1024)S(1)} %add_rsqrt_fusion, f32[4096,256]{1,0:T(8,128)} %get-tuple-element.11, f32[256]{0:T(256)S(1)} %pmax.7), kind=kOutput, calls=%fused_computation.12 | convolution fusion | flops 2166358016 | bytes 13652992 | tf_op jit(solution)/shard_map/dot_general | solution.py:19
  94.8 0.0 all-reduce.4.cloned.1.call-start
  94.8 37.9 %reduce-scatter.2.cloned.1.call-done = f32[32,1024]{1,0:T(8,128)} async-done(((f32[256,1024]{1,0:T(8,128)}), f32[32,1024]{1,0:T(8,128)}) %reduce-scatter.2.cloned.1.call-update) | async-done | bytes 131088 | tf_op jit(solution)/shard_map/reduce_scatter | solution.py:24
  132.7 0.0 all-reduce.4.cloned.1.call-update
  132.8 0.0 all-reduce.6.cloned.1.call-start
  132.8 3.4 fusion.3
  136.2 0.6 dynamic-slice
  137.4 16.9 %all-reduce = f32[256]{0:T(256)S(1)} all-reduce(f32[256]{0:T(256)S(1)} %get-tuple-element.6), channel_id=3, replica_groups=mesh['seq'=16,'exp'=8] {'exp'}, use_global_device_ids=true, to_apply=%region_8.0.clone | all-reduce | flops 256 | bytes 2048
  154.4 0.1 dynamic-slice.1
  154.4 33.1 %psum.22 = f32[32]{0:T(128)S(1)} all-reduce(f32[32]{0:T(128)S(1)} %dynamic-slice.1), channel_id=1, replica_groups=mesh['seq'=16,'exp'=8] {'seq'}, use_global_device_ids=true, to_apply=%region_9.0 | all-reduce | flops 32 | bytes 256 | tf_op jit(solution)/shard_map/psum | solution.py:27
  187.6 85.0 %all-reduce.4.cloned.1.call-done = f32[32,1024]{1,0:T(8,128)} async-done(((f32[32,1024]{1,0:T(8,128)}), f32[32,1024]{1,0:T(8,128)}) %all-reduce.4.cloned.1.call-update) | async-done | bytes 131088 | tf_op jit(solution)/shard_map/psum | solution.py:27
  272.5 1.0 divide_convert_fusion.2
  273.6 3.0 fusion.55
  276.6 0.4 copy-done.2
  277.0 0.7 convolution_convert_fusion.1
  277.7 0.7 convert_element_type.34
  278.4 130.1 %all-reduce.6.cloned.1.call-done = bf16[32,1024]{1,0:T(8,128)(2,1)} async-done(((bf16[32,1024]{1,0:T(8,128)(2,1)}), bf16[32,1024]{1,0:T(8,128)(2,1)}) %all-reduce.6.cloned.1.call-update) | async-done | bytes 65552 | tf_op jit(solution)/shard_map/psum | solution.py:36
  408.5 0.9 stack.2
  409.3 13.8 %all_to_all.5 = bf16[8,32,1024]{2,1,0:T(8,128)(2,1)S(1)} all-to-all(bf16[8,32,1024]{2,1,0:T(8,128)(2,1)S(1)} %stack.2), channel_id=1, replica_groups=mesh['seq'=16,'exp'=8] {'exp'}, dimensions={0} | all-to-all | bytes 1048576 | tf_op jit(solution)/shard_map/all_to_all | solution.py:38
  423.1 6.4 %convolution_convert_fusion = bf16[4096,1024]{1,0:T(8,128)(2,1)} fusion(bf16[256,1024]{1,0:T(8,128)(2,1)S(1)} %bitcast.7, f32[4096,256]{1,0:T(8,128)} %get-tuple-element.11, f32[4096]{0:T(1024)S(1)} %get-tuple-element.5, f32[4096]{0:T(1024)S(1)} %get-tuple-element.7), kind=kOutput, calls=%fused_computation.5 | convolution fusion | flops 2154823680 | bytes 13139968 | tf_op jit(solution)/shard_map/dot_general | solution.py:43
  (13 shorter events, 0.1 us)
Async XLA Ops:
  6.5 5.3 %copy-start = (bf16[1024,256]{1,0:T(8,128)(2,1)S(1)}, bf16[1024,256]{1,0:T(8,128)(2,1)}, u32[]{:S(2)}) copy-start(bf16[1024,256]{1,0:T(8,128)(2,1)} %param.7) | copy-start | bytes 1572868
  6.5 5.3 %copy-start.3 = (f32[1024]{0:T(1024)S(1)}, f32[1024]{0:T(1024)}, u32[]{:S(2)}) copy-start(f32[1024]{0:T(1024)} %param.6) | copy-start | bytes 12292
  6.5 126.2 %reduce-scatter.2.cloned.1.call-start = ((), (), s32[]{:S(2)}) async-start(), calls=%async_computation.2 | async-start | bytes 1179648 | tf_op jit(solution)/shard_map/reduce_scatter | solution.py:24
  6.5 6.0 %copy-start.1 = (bf16[4096,1024]{1,0:T(8,128)(2,1)S(1)}, bf16[4096,1024]{1,0:T(8,128)(2,1)}, u32[]{:S(2)}) copy-start(bf16[4096,1024]{1,0:T(8,128)(2,1)} %param.5) | copy-start | bytes 25165828
  94.8 41.4 %copy-start.4 = (u32[128]{0:T(128)S(1)}, u32[128]{0:T(128)}, u32[]{:S(2)}) copy-start(u32[128]{0:T(128)} %constant.70) | copy-start | bytes 1540
  94.8 177.8 %all-reduce.4.cloned.1.call-start = ((), (), s32[]{:S(2)}) async-start(), calls=%async_computation.3 | async-start | bytes 262144 | tf_op jit(solution)/shard_map/psum | solution.py:27
  132.8 275.7 %all-reduce.6.cloned.1.call-start = ((), (), s32[]{:S(2)}) async-start(), calls=%async_computation.4 | async-start | bytes 131072 | tf_op jit(solution)/shard_map/psum | solution.py:36
  273.6 3.5 copy-start.2
Sparse Core Ops, SparseCore 0:
  94.9 37.7 reduce-scatter.1
  135.2 137.2 all-reduce.3
  278.5 129.9 all-reduce.5
